TPU v7x, 32 devices: a whole 2x2x4 slice. The times are simulated.
32 devices in a mesh: region: 16 (over z, y, core), panel: 2 (over x).
Axes of the slice: x: 2, y: 2, z: 4, core: 2. Of those that a mesh axis runs over, the one named last changes fastest.
Arguments:
- multipliers: bfloat16 [16, 4096, 512], P('region', 'panel'), may hold values from -6 to 6
- flexibility: bfloat16 [16, 4096, 4096], P('region', 'panel'), as said below
- interface_sizes: int32 [16], P('region'), may hold values from 1024 to 4096, as said below
- send_rows: int32 [16, 2, 1536], replicated, may hold values from 0 to 4095, as said below
- recv_rows: int32 [16, 2, 1536], P('region'), may hold values from 0 to 4095, as said below
- recv_pos: int32 [16, 2, 1536], P('region'), may hold values from 0 to 1534
- recv_weight: float32 [16, 2, 1536], P('region'), may hold values from 0 to 1
Outputs:
- dual_image: float32 [16, 4096, 512], P('region', None, 'panel')
Inputs may be any that keep to these rules, and one draw needn't show every extreme that they name: `flexibility`: each region's matrix is symmetric. `interface_sizes`: A multiple of 128. `send_rows`: every entry of region r is below interface_sizes[r]; side 0 faces region r - 1 and side 1 region r + 1 around the loop; rows may repeat. `recv_rows`: every entry of region r is below interface_sizes[r]; rows may repeat.
All inputs are finite; a program needn't handle non-finite values.
Results may differ from a plain program's by a relative error of at most 0.0029.
Values may be sent and summed in bfloat16 or wider, within the bound.
No kernel may reach another device: no remote copies, remote signals or barrier semaphores. Data moves between devices by JAX's collectives and lax.ppermute only.
A program may use at most 128 MiB of HBM per device.

v0:
```python
import jax
import jax.numpy as jnp
from jax import lax
from jax.sharding import PartitionSpec as P


def shifted(value, axis, steps):
    count = lax.axis_size(axis)
    pairs = [(source, (source + steps) % count) for source in range(count)]
    return lax.ppermute(value, axis, pairs)


def interpolate(arrived, position, weight):
    first_rows = arrived[position].astype(jnp.float32)
    second_rows = arrived[position + 1].astype(jnp.float32)
    return (1.0 - weight)[:, None] * first_rows + weight[:, None] * second_rows


def on_device(
    multipliers, flexibility, interface_sizes, send_rows, recv_rows, recv_pos, recv_weight
):
    local_block = multipliers[0]
    flex_panel = flexibility[0]
    rows_here = local_block.shape[0]
    first_row = lax.axis_index("panel") * rows_here
    row_ids = first_row + jnp.arange(rows_here, dtype=jnp.int32)
    live_here = (row_ids < interface_sizes[0])[:, None]
    live_block = jnp.where(live_here, local_block, jnp.zeros((), local_block.dtype))
    image = jnp.dot(
        flex_panel,
        lax.all_gather(live_block, "panel", axis=0, tiled=True),
        preferred_element_type=jnp.float32,
    )
    settled = jnp.where(live_here, image, jnp.zeros((), image.dtype)).astype(jnp.bfloat16)
    columns_all = lax.all_to_all(settled, "panel", split_axis=1, concat_axis=0, tiled=True)
    region_index = lax.axis_index("region")
    regions = lax.axis_size("region")
    lower_region = (region_index + regions - 1) % regions
    upper_region = (region_index + 1) % regions
    lower_all = shifted(columns_all, "region", 1)
    upper_all = shifted(columns_all, "region", -1)
    from_lower = lower_all[send_rows[lower_region, 1]]
    from_upper = upper_all[send_rows[upper_region, 0]]
    jump_lower = interpolate(from_lower, recv_pos[0, 0], recv_weight[0, 0])
    jump_upper = interpolate(from_upper, recv_pos[0, 1], recv_weight[0, 1])
    jumps = jnp.concatenate([jump_lower, jump_upper], axis=0)
    targets = recv_rows[0].reshape(-1)
    result = columns_all.astype(jnp.float32).at[targets].add(-jumps)
    return result[None]


def solution(mesh):
    in_specs = (
        P("region", "panel", None),
        P("region", "panel", None),
        P("region"),
        P(),
        P("region", None, None),
        P("region", None, None),
        P("region", None, None),
    )
    out_specs = P("region", None, "panel")
    return jax.shard_map(
        on_device, mesh=mesh, in_specs=in_specs, out_specs=out_specs, check_vma=False
    )
```

profile of v0, /device:TPU:1, one launch (start us, length us, event | category | flops | bytes accessed | tf_op | source)
XLA Modules:
  0.0 225.4 jit_solution(8095538490072219212)
XLA Ops:
  6.5 0.0 all-gather.2.cloned.1.call-start
  7.2 2.8 %bitcast_select_fusion = bf16[2048,512]{1,0:T(8,128)(2,1)} fusion(bf16[1,2048,512]{2,1,0:T(8,128)(2,1)} %param.7, pred[2048]{0:T(1024)(128)(4,1)S(1)} %add_compare_fusion), kind=kLoop, calls=%fused_computation.14 | loop fusion | flops 1048576 | bytes 4196352 | tf_op jit(solution)/shard_map/jit(_where)/select_n | solution.py:28
  10.0 0.0 all-gather.2.cloned.1.call-update
  10.0 58.8 %all-gather.2.cloned.1.call-done = bf16[4096,512]{1,0:T(8,128)(2,1)} async-done(((bf16[2048,512]{1,0:T(8,128)(2,1)}), bf16[4096,512]{1,0:T(8,128)(2,1)}) %all-gather.2.cloned.1.call-update) | async-done | bytes 4194320 | tf_op jit(solution)/shard_map/all_gather | solution.py:31
  68.8 14.7 %select_convert_fusion = bf16[512,2048]{1,0:T(8,128)(2,1)} fusion(bf16[4096,512]{1,0:T(8,128)(2,1)} %all-gather.2.cloned.1.call-done, bf16[1,2048,4096]{2,1,0:T(8,128)(2,1)} %param.8, pred[2048]{0:T(1024)(128)(4,1)S(1)} %add_compare_fusion), kind=kOutput, calls=%fused_computation.9 | convolution fusion | flops 8592031744 | bytes 23070720 | tf_op jit(solution)/shard_map/dot_general | solution.py:29
  83.4 3.9 %all-to-all-start = ((bf16[2048,2,256]{0,2,1:T(8,128)(2,1)}), bf16[2048,2,256]{0,2,1:T(8,128)(2,1)S(1)}, u32[]{:S(2)}, u32[]{:S(2)}) async-start(bf16[2048,2,256]{0,2,1:T(8,128)(2,1)} %bitcast.42), calls=%async_computation | async-start | bytes 4194304 | tf_op jit(solution)/shard_map/all_to_all | solution.py:35
  87.4 0.8 fusion.7
  88.2 0.1 fusion.8
  88.3 23.1 %all-to-all-done = bf16[2048,2,256]{0,2,1:T(8,128)(2,1)S(1)} async-done(((bf16[2048,2,256]{0,2,1:T(8,128)(2,1)}), bf16[2048,2,256]{0,2,1:T(8,128)(2,1)S(1)}, u32[]{:S(2)}, u32[]{:S(2)}) %all-to-all-start) | async-done | bytes 2097184 | tf_op jit(solution)/shard_map/all_to_all | solution.py:35
  111.4 2.5 %copy.9 = bf16[2,2048,256]{2,1,0:T(8,128)(2,1)} copy(bf16[2,2048,256]{1,2,0:T(8,128)(2,1)S(1)} %bitcast.41) | data formatting | bytes 4194304 | tf_op jit(solution)/shard_map/all_to_all | solution.py:35
  113.9 2.8 %collective-permute-start = (bf16[4096,256]{1,0:T(8,128)(2,1)}, bf16[4096,256]{1,0:T(8,128)(2,1)}, u32[]{:S(2)}, u32[]{:S(2)}) collective-permute-start(bf16[4096,256]{1,0:T(8,128)(2,1)} %bitcast.6), channel_id=1, source_target_pairs={{0,2},{2,4},{4,6},{6,8},{8,10},{10,12},{12,14},{14,16},{16,18},{18... | collective-permute-start | bytes 6291464 | tf_op jit(solution)/shard_map/ppermute | solution.py:10
  116.7 0.0 collective-permute-start.1
  116.8 3.9 %bitcast_convert_fusion = f32[4096,256]{1,0:T(8,128)} fusion(bf16[2,2048,256]{2,1,0:T(8,128)(2,1)} %copy.9), kind=kLoop, calls=%fused_computation.45 | loop fusion | flops 1048576 | bytes 6291456 | tf_op jit(solution)/shard_map/convert_element_type | solution.py:48
  120.7 41.7 %collective-permute-done = bf16[4096,256]{1,0:T(8,128)(2,1)} collective-permute-done((bf16[4096,256]{1,0:T(8,128)(2,1)}, bf16[4096,256]{1,0:T(8,128)(2,1)}, u32[]{:S(2)}, u32[]{:S(2)}) %collective-permute-start) | collective-permute-done | bytes 2097184 | tf_op jit(solution)/shard_map/ppermute | solution.py:10
  162.4 5.5 %gather_fusion = bf16[1536,256]{1,0:T(8,128)(2,1)S(1)} fusion(bf16[4096,256]{1,0:T(8,128)(2,1)} %collective-permute-done, s32[2048]{0:T(1024)S(1)} %pad_clamp_fusion.5), kind=kCustom, calls=%fused_computation | custom fusion | bytes 1579008 | tf_op jit(solution)/shard_map/gather | solution.py:42
  168.0 5.4 %gather_fusion.1 = bf16[1536,256]{1,0:T(8,128)(2,1)} fusion(bf16[1536,256]{1,0:T(8,128)(2,1)S(1)} %gather_fusion, s32[2048]{0:T(1024)S(1)} %get-tuple-element.16), kind=kCustom, calls=%fused_computation.1 | custom fusion | bytes 1579008 | tf_op jit(solution)/shard_map/gather | solution.py:14
  173.3 5.4 %gather_fusion.2 = bf16[1536,256]{1,0:T(8,128)(2,1)} fusion(bf16[1536,256]{1,0:T(8,128)(2,1)S(1)} %gather_fusion, s32[2048]{0:T(1024)S(1)} %get-tuple-element.15), kind=kCustom, calls=%fused_computation.2 | custom fusion | bytes 1579008 | tf_op jit(solution)/shard_map/gather | solution.py:15
  178.7 0.0 collective-permute-done.1
  178.7 4.8 %gather_fusion.3 = bf16[1536,256]{1,0:T(8,128)(2,1)S(1)} fusion(bf16[4096,256]{1,0:T(8,128)(2,1)S(1)} %collective-permute-done.1, s32[2048]{0:T(1024)S(1)} %pad_clamp_fusion.2), kind=kCustom, calls=%fused_computation.3 | custom fusion | bytes 1579008 | tf_op jit(solution)/shard_map/gather | solution.py:43
  183.4 5.4 %gather_fusion.4 = bf16[1536,256]{1,0:T(8,128)(2,1)} fusion(bf16[1536,256]{1,0:T(8,128)(2,1)S(1)} %gather_fusion.3, s32[2048]{0:T(1024)S(1)} %get-tuple-element.14), kind=kCustom, calls=%fused_computation.4 | custom fusion | bytes 1579008 | tf_op jit(solution)/shard_map/gather | solution.py:14
  188.8 5.3 %gather_fusion.5 = bf16[1536,256]{1,0:T(8,128)(2,1)} fusion(bf16[1536,256]{1,0:T(8,128)(2,1)S(1)} %gather_fusion.3, s32[2048]{0:T(1024)S(1)} %get-tuple-element.13), kind=kCustom, calls=%fused_computation.5 | custom fusion | bytes 1579008 | tf_op jit(solution)/shard_map/gather | solution.py:15
  194.1 2.0 multiply_add_fusion.1
  196.1 0.5 multiply_add_fusion
  196.6 22.0 %scatter_custom_fusion = f32[4096,256]{1,0:T(8,128)} fusion(f32[4096,256]{1,0:T(8,128)} %bitcast_convert_fusion, s32[3072]{0:T(1024)S(1)} %bitcast.45, f32[1536,256]{1,0:T(8,128)S(1)} %multiply_add_fusion, f32[]{:T(128)} %constant.63, f32[1536,256]{1,0:T(8,128)S(1)} %multiply_add_fusion.1), kind=kCustom, calls=%fused_computation.11 | custom fusion | flops 2359296 | bytes 7340544 | tf_op jit(solution)/shard_map/scatter-add | solution.py:48
  (19 shorter events, 0.1 us)
Async XLA Ops:
  6.5 62.2 %all-gather.2.cloned.1.call-start = ((), (), s32[]{:S(2)}) async-start(), calls=%async_computation.1 | async-start | bytes 6291456 | tf_op jit(solution)/shard_map/all_gather | solution.py:31
  83.4 4.7 %copy-start.4 = (s32[1,2,1536]{2,1,0:T(2,128)S(1)}, s32[1,2,1536]{2,1,0:T(2,128)}, u32[]{:S(2)}) copy-start(s32[1,2,1536]{2,1,0:T(2,128)} %param.12) | copy-start | bytes 36868
  83.4 28.0 %all-to-all-start = ((bf16[2048,2,256]{0,2,1:T(8,128)(2,1)}), bf16[2048,2,256]{0,2,1:T(8,128)(2,1)S(1)}, u32[]{:S(2)}, u32[]{:S(2)}) async-start(bf16[2048,2,256]{0,2,1:T(8,128)(2,1)} %bitcast.42), calls=%async_computation | async-start | bytes 4194304 | tf_op jit(solution)/shard_map/all_to_all | solution.py:35
  111.4 5.3 %copy-start.3 = (s32[1,2,1536]{2,1,0:T(2,128)S(1)}, s32[1,2,1536]{2,1,0:T(2,128)}, u32[]{:S(2)}) copy-start(s32[1,2,1536]{2,1,0:T(2,128)} %param.11) | copy-start | bytes 36868
  111.4 5.3 %copy-start.2 = (f32[1,2,1536]{2,1,0:T(2,128)S(1)}, f32[1,2,1536]{2,1,0:T(2,128)}, u32[]{:S(2)}) copy-start(f32[1,2,1536]{2,1,0:T(2,128)} %param.13) | copy-start | bytes 36868
  113.9 48.5 %collective-permute-start = (bf16[4096,256]{1,0:T(8,128)(2,1)}, bf16[4096,256]{1,0:T(8,128)(2,1)}, u32[]{:S(2)}, u32[]{:S(2)}) collective-permute-start(bf16[4096,256]{1,0:T(8,128)(2,1)} %bitcast.6), channel_id=1, source_target_pairs={{0,2},{2,4},{4,6},{6,8},{8,10},{10,12},{12,14},{14,16},{16,18},{18... | collective-permute-start | bytes 6291464 | tf_op jit(solution)/shard_map/ppermute | solution.py:10
  116.7 62.0 %collective-permute-start.1 = (bf16[4096,256]{1,0:T(8,128)(2,1)}, bf16[4096,256]{1,0:T(8,128)(2,1)S(1)}, u32[]{:S(2)}, u32[]{:S(2)}) collective-permute-start(bf16[4096,256]{1,0:T(8,128)(2,1)} %bitcast.6), channel_id=1, source_target_pairs={{0,30},{2,0},{4,2},{6,4},{8,6},{10,8},{12,10},{14,12},{16,14},{18,... | collective-permute-start | bytes 6291464 | tf_op jit(solution)/shard_map/ppermute | solution.py:10
  194.1 2.0 copy-start
  194.1 2.0 copy-start.1
Sparse Core Ops, SparseCore 0:
  10.1 58.6 all-gather.1
where the time goes:
time: 226 us; the launch traced here: 225 us
  waiting for transfers between devices  124 us (55%)
  local copies, waits for them, and re-layouts  34.2 us (15%)
  other arithmetic  32 us (14%)
  matrix products  14.7 us (7%)
  between operations  14.2 us (6%)
  starting transfers between devices  6.68 us (3%)
    all_gather x1, waiting for transfers between devices, on_device(): lax.all_gather(live_block, 'panel', axis=0, tiled=True)  58.8 us
    ppermute x2, waiting for transfers between devices, shifted(): return lax.ppermute(value, axis, pairs)  41.7 us
    all_to_all x1, waiting for transfers between devices, on_device(): lax.all_to_all(settled, 'panel', split_axis=1, concat_axis=0, tiled=True)  23.1 us
    scatter-add x1, other arithmetic, on_device(): result = columns_all.astype(jnp.float32).at[targets].add(-jumps)  22 us
    dot_general x1, matrix products, on_device(): jnp.dot(flex_panel, lax.all_gather(live_block, 'panel', axis=0, tiled=Tru...  14.7 us
    gather x2, local copies, waits for them, and re-layouts, interpolate(): first_rows = arrived[position].astype(jnp.float32)  10.7 us
    gather x2, local copies, waits for them, and re-layouts, interpolate(): second_rows = arrived[position + 1].astype(jnp.float32)  10.7 us
    gather x1, local copies, waits for them, and re-layouts, on_device(): from_lower = lower_all[send_rows[lower_region, 1]]  5.51 us
  transfers between devices with their start and end apart: 4, of which 3 were waited for; matrix products, arithmetic and copies ran while one was open for 9% of the time, Pallas kernels for 0%

commit v1 on v0

--- a/solution.py
+++ b/solution.py
@@ -2,6 +2,18 @@
 import jax.numpy as jnp
 from jax import lax
 from jax.sharding import PartitionSpec as P
+
+
+def doubled_up(x, axis, dim):
+    ways, here, turn = (lax.axis_size(axis), lax.axis_index(axis), x.shape[dim])
+    line, have = (x, 1)
+    while have < ways:
+        line = jnp.concatenate(
+            [line, lax.ppermute(line, axis, [(d, (d - have) % ways) for d in range(ways)])],
+            axis=dim,
+        )
+        have = 2 * have
+    return jnp.roll(line, here * turn, axis=dim)
 
 
 def shifted(value, axis, steps):
@@ -27,9 +39,7 @@
     live_here = (row_ids < interface_sizes[0])[:, None]
     live_block = jnp.where(live_here, local_block, jnp.zeros((), local_block.dtype))
     image = jnp.dot(
-        flex_panel,
-        lax.all_gather(live_block, "panel", axis=0, tiled=True),
-        preferred_element_type=jnp.float32,
+        flex_panel, doubled_up(live_block, "panel", 0), preferred_element_type=jnp.float32
     )
     settled = jnp.where(live_here, image, jnp.zeros((), image.dtype)).astype(jnp.bfloat16)
     columns_all = lax.all_to_all(settled, "panel", split_axis=1, concat_axis=0, tiled=True)

time: 226 us -> 207 us (0.916)
  waiting for transfers between devices: 124 us -> 110 us
  between operations: 14.2 us -> 0.86 us
  matrix products: 14.7 us -> 21.9 us
  starting transfers between devices: 6.68 us -> 9.18 us
    all_gather x1 -> x0, waiting for transfers between devices: 58.8 us -> none  [on_device(): lax.all_gather(live_block, 'panel', axis=0, tiled=True)]
    ppermute x0 -> x1, waiting for transfers between devices: none -> 45.4 us  [doubled_up(): lax.ppermute(line, axis, [(d, (d - have) % ways) for d in range(ways)])]
    dot_general x1, matrix products: 14.7 us -> 21.9 us  [on_device(): jnp.dot(flex_panel, doubled_up(live_block, 'panel', 0), preferred_element...]
  transfers between devices with their start and end apart: 4 -> 4, of which waited for: 3 -> 3; matrix products, arithmetic and copies ran while one was open for 9% -> 10% of each run, Pallas kernels for 0% -> 0%
where the time goes in v1:
time: 207 us
  waiting for transfers between devices  110 us (53%)
  local copies, waits for them, and re-layouts  34.2 us (17%)
  other arithmetic  31.1 us (15%)
  matrix products  21.9 us (11%)
  starting transfers between devices  9.18 us (4%)
    ppermute x1, waiting for transfers between devices, doubled_up(): lax.ppermute(line, axis, [(d, (d - have) % ways) for d in range(ways)])  45.4 us
    ppermute x2, waiting for transfers between devices, shifted(): return lax.ppermute(value, axis, pairs)  41.7 us
    all_to_all x1, waiting for transfers between devices, on_device(): lax.all_to_all(settled, 'panel', split_axis=1, concat_axis=0, tiled=True)  22.7 us
    scatter-add x1, other arithmetic, on_device(): result = columns_all.astype(jnp.float32).at[targets].add(-jumps)  22 us
    dot_general x1, matrix products, on_device(): jnp.dot(flex_panel, doubled_up(live_block, 'panel', 0), preferred_element...  21.9 us
    gather x2, local copies, waits for them, and re-layouts, interpolate(): first_rows = arrived[position].astype(jnp.float32)  10.7 us
    gather x2, local copies, waits for them, and re-layouts, interpolate(): second_rows = arrived[position + 1].astype(jnp.float32)  10.7 us
    gather x1, local copies, waits for them, and re-layouts, on_device(): from_lower = lower_all[send_rows[lower_region, 1]]  5.51 us
  transfers between devices with their start and end apart: 4, of which 3 were waited for; matrix products, arithmetic and copies ran while one was open for 10% of the time, Pallas kernels for 0%

profile of v1, /device:TPU:1, one launch (start us, length us, event | category | flops | bytes accessed | tf_op | source)
XLA Modules:
  0.0 207.0 jit_solution(6537777028410654272)
XLA Ops:
  0.7 1.8 bitcast_select_fusion
  2.4 2.1 %collective-permute-start = (bf16[2048,512]{1,0:T(8,128)(2,1)S(1)}, bf16[2048,512]{1,0:T(8,128)(2,1)}, u32[]{:S(2)}, u32[]{:S(2)}) collective-permute-start(bf16[2048,512]{1,0:T(8,128)(2,1)S(1)} %bitcast_select_fusion), channel_id=1, source_target_pairs={{0,1},{1,0},{2,3},{3,2},{4,5},{5,4},{6,7},{7,6},{8,9},{9,8},{10,11... | collective-permute-start | bytes 6291464 | tf_op jit(solution)/shard_map/ppermute | solution.py:12
  4.5 45.4 %collective-permute-done = bf16[2048,512]{1,0:T(8,128)(2,1)} collective-permute-done((bf16[2048,512]{1,0:T(8,128)(2,1)S(1)}, bf16[2048,512]{1,0:T(8,128)(2,1)}, u32[]{:S(2)}, u32[]{:S(2)}) %collective-permute-start) | collective-permute-done | bytes 2097184 | tf_op jit(solution)/shard_map/ppermute | solution.py:12
  50.0 21.9 %select_convert_fusion = bf16[512,2048]{1,0:T(8,128)(2,1)} fusion(bf16[1,2048,4096]{2,1,0:T(8,128)(2,1)} %param.8, s32[]{:T(128)S(6)} %select_n.110, bf16[2048,512]{1,0:T(8,128)(2,1)S(1)} %bitcast_select_fusion, bf16[2048,512]{1,0:T(8,128)(2,1)} %collective-permute-done, pred[2048]{0:T(1024)(128)(4,1)S(1)} %add_compare_fusion), kind=kOutput, calls=%fused_computation.16 | convolution fusion | flops 8608808960 | bytes 23070724 | tf_op jit(solution)/shard_map/dot_general | solution.py:41
  71.9 3.9 %all-to-all-start = ((bf16[2048,2,256]{0,2,1:T(8,128)(2,1)}), bf16[2048,2,256]{0,2,1:T(8,128)(2,1)S(1)}, u32[]{:S(2)}, u32[]{:S(2)}) async-start(bf16[2048,2,256]{0,2,1:T(8,128)(2,1)} %bitcast.41), calls=%async_computation | async-start | bytes 4194304 | tf_op jit(solution)/shard_map/all_to_all | solution.py:45
  75.8 0.0 copy-start.3
  75.8 0.0 copy-start.2
  75.8 0.8 fusion.13
  76.6 0.1 fusion.14
  76.7 22.7 %all-to-all-done = bf16[2048,2,256]{0,2,1:T(8,128)(2,1)S(1)} async-done(((bf16[2048,2,256]{0,2,1:T(8,128)(2,1)}), bf16[2048,2,256]{0,2,1:T(8,128)(2,1)S(1)}, u32[]{:S(2)}, u32[]{:S(2)}) %all-to-all-start) | async-done | bytes 2097184 | tf_op jit(solution)/shard_map/all_to_all | solution.py:45
  99.4 2.5 %copy.9 = bf16[2,2048,256]{2,1,0:T(8,128)(2,1)} copy(bf16[2,2048,256]{1,2,0:T(8,128)(2,1)S(1)} %bitcast.40) | data formatting | bytes 4194304 | tf_op jit(solution)/shard_map/all_to_all | solution.py:45
  101.9 3.2 %collective-permute-start.1 = (bf16[4096,256]{1,0:T(8,128)(2,1)}, bf16[4096,256]{1,0:T(8,128)(2,1)}, u32[]{:S(2)}, u32[]{:S(2)}) collective-permute-start(bf16[4096,256]{1,0:T(8,128)(2,1)} %bitcast.6), channel_id=1, source_target_pairs={{0,2},{2,4},{4,6},{6,8},{8,10},{10,12},{12,14},{14,16},{16,18},{18... | collective-permute-start | bytes 6291464 | tf_op jit(solution)/shard_map/ppermute | solution.py:22
  105.1 0.0 collective-permute-start.2
  105.3 3.9 %bitcast_convert_fusion = f32[4096,256]{1,0:T(8,128)} fusion(bf16[2,2048,256]{2,1,0:T(8,128)(2,1)} %copy.9), kind=kLoop, calls=%fused_computation.54 | loop fusion | flops 1048576 | bytes 6291456 | tf_op jit(solution)/shard_map/convert_element_type | solution.py:58
  109.2 41.7 %collective-permute-done.1 = bf16[4096,256]{1,0:T(8,128)(2,1)} collective-permute-done((bf16[4096,256]{1,0:T(8,128)(2,1)}, bf16[4096,256]{1,0:T(8,128)(2,1)}, u32[]{:S(2)}, u32[]{:S(2)}) %collective-permute-start.1) | collective-permute-done | bytes 2097184 | tf_op jit(solution)/shard_map/ppermute | solution.py:22
  150.9 5.5 %gather_fusion = bf16[1536,256]{1,0:T(8,128)(2,1)S(1)} fusion(bf16[4096,256]{1,0:T(8,128)(2,1)} %collective-permute-done.1, s32[2048]{0:T(1024)S(1)} %pad_clamp_fusion.5), kind=kCustom, calls=%fused_computation | custom fusion | bytes 1579008 | tf_op jit(solution)/shard_map/gather | solution.py:52
  156.4 5.4 %gather_fusion.1 = bf16[1536,256]{1,0:T(8,128)(2,1)} fusion(bf16[1536,256]{1,0:T(8,128)(2,1)S(1)} %gather_fusion, s32[2048]{0:T(1024)S(1)} %get-tuple-element.16), kind=kCustom, calls=%fused_computation.1 | custom fusion | bytes 1579008 | tf_op jit(solution)/shard_map/gather | solution.py:26
  161.8 5.4 %gather_fusion.2 = bf16[1536,256]{1,0:T(8,128)(2,1)} fusion(bf16[1536,256]{1,0:T(8,128)(2,1)S(1)} %gather_fusion, s32[2048]{0:T(1024)S(1)} %get-tuple-element.15), kind=kCustom, calls=%fused_computation.2 | custom fusion | bytes 1579008 | tf_op jit(solution)/shard_map/gather | solution.py:27
  167.1 4.8 %gather_fusion.3 = bf16[1536,256]{1,0:T(8,128)(2,1)S(1)} fusion(bf16[4096,256]{1,0:T(8,128)(2,1)S(1)} %collective-permute-done.2, s32[2048]{0:T(1024)S(1)} %pad_clamp_fusion.2), kind=kCustom, calls=%fused_computation.3 | custom fusion | bytes 1579008 | tf_op jit(solution)/shard_map/gather | solution.py:53
  171.9 5.4 %gather_fusion.4 = bf16[1536,256]{1,0:T(8,128)(2,1)} fusion(bf16[1536,256]{1,0:T(8,128)(2,1)S(1)} %gather_fusion.3, s32[2048]{0:T(1024)S(1)} %get-tuple-element.14), kind=kCustom, calls=%fused_computation.4 | custom fusion | bytes 1579008 | tf_op jit(solution)/shard_map/gather | solution.py:26
  177.2 5.3 %gather_fusion.5 = bf16[1536,256]{1,0:T(8,128)(2,1)} fusion(bf16[1536,256]{1,0:T(8,128)(2,1)S(1)} %gather_fusion.3, s32[2048]{0:T(1024)S(1)} %get-tuple-element.13), kind=kCustom, calls=%fused_computation.5 | custom fusion | bytes 1579008 | tf_op jit(solution)/shard_map/gather | solution.py:27
  182.6 2.0 multiply_add_fusion.1
  184.6 0.5 multiply_add_fusion
  185.0 22.0 %scatter_custom_fusion = f32[4096,256]{1,0:T(8,128)} fusion(f32[4096,256]{1,0:T(8,128)} %bitcast_convert_fusion, s32[3072]{0:T(1024)S(1)} %bitcast.44, f32[1536,256]{1,0:T(8,128)S(1)} %multiply_add_fusion, f32[]{:T(128)} %constant.83, f32[1536,256]{1,0:T(8,128)S(1)} %multiply_add_fusion.1), kind=kCustom, calls=%fused_computation.18 | custom fusion | flops 2359296 | bytes 7340544 | tf_op jit(solution)/shard_map/scatter-add | solution.py:58
  (18 shorter events, 0.1 us)
Async XLA Ops:
  2.4 47.5 %collective-permute-start = (bf16[2048,512]{1,0:T(8,128)(2,1)S(1)}, bf16[2048,512]{1,0:T(8,128)(2,1)}, u32[]{:S(2)}, u32[]{:S(2)}) collective-permute-start(bf16[2048,512]{1,0:T(8,128)(2,1)S(1)} %bitcast_select_fusion), channel_id=1, source_target_pairs={{0,1},{1,0},{2,3},{3,2},{4,5},{5,4},{6,7},{7,6},{8,9},{9,8},{10,11... | collective-permute-start | bytes 6291464 | tf_op jit(solution)/shard_map/ppermute | solution.py:12
  71.9 4.8 %copy-start.4 = (s32[1,2,1536]{2,1,0:T(2,128)S(1)}, s32[1,2,1536]{2,1,0:T(2,128)}, u32[]{:S(2)}) copy-start(s32[1,2,1536]{2,1,0:T(2,128)} %param.12) | copy-start | bytes 36868
  71.9 27.6 %all-to-all-start = ((bf16[2048,2,256]{0,2,1:T(8,128)(2,1)}), bf16[2048,2,256]{0,2,1:T(8,128)(2,1)S(1)}, u32[]{:S(2)}, u32[]{:S(2)}) async-start(bf16[2048,2,256]{0,2,1:T(8,128)(2,1)} %bitcast.41), calls=%async_computation | async-start | bytes 4194304 | tf_op jit(solution)/shard_map/all_to_all | solution.py:45
  75.8 29.4 %copy-start.3 = (s32[1,2,1536]{2,1,0:T(2,128)S(1)}, s32[1,2,1536]{2,1,0:T(2,128)}, u32[]{:S(2)}) copy-start(s32[1,2,1536]{2,1,0:T(2,128)} %param.11) | copy-start | bytes 36868
  75.8 29.4 %copy-start.2 = (f32[1,2,1536]{2,1,0:T(2,128)S(1)}, f32[1,2,1536]{2,1,0:T(2,128)}, u32[]{:S(2)}) copy-start(f32[1,2,1536]{2,1,0:T(2,128)} %param.13) | copy-start | bytes 36868
  101.9 49.0 %collective-permute-start.1 = (bf16[4096,256]{1,0:T(8,128)(2,1)}, bf16[4096,256]{1,0:T(8,128)(2,1)}, u32[]{:S(2)}, u32[]{:S(2)}) collective-permute-start(bf16[4096,256]{1,0:T(8,128)(2,1)} %bitcast.6), channel_id=1, source_target_pairs={{0,2},{2,4},{4,6},{6,8},{8,10},{10,12},{12,14},{14,16},{16,18},{18... | collective-permute-start | bytes 6291464 | tf_op jit(solution)/shard_map/ppermute | solution.py:22
  105.1 62.0 %collective-permute-start.2 = (bf16[4096,256]{1,0:T(8,128)(2,1)}, bf16[4096,256]{1,0:T(8,128)(2,1)S(1)}, u32[]{:S(2)}, u32[]{:S(2)}) collective-permute-start(bf16[4096,256]{1,0:T(8,128)(2,1)} %bitcast.6), channel_id=1, source_target_pairs={{0,30},{2,0},{4,2},{6,4},{8,6},{10,8},{12,10},{14,12},{16,14},{18,... | collective-permute-start | bytes 6291464 | tf_op jit(solution)/shard_map/ppermute | solution.py:22
  182.6 2.0 copy-start
  182.6 2.0 copy-start.1
